TPU v7x, 512 devices: a whole 4x8x8 slice. The times are simulated.
512 devices in a mesh: pages: 64 (over y, z_lo, core), heads: 8 (over x, z_hi).
Axes of the slice: x: 4, y: 8, z: 8 (z_hi: 2, z_lo: 4; z = z_hi * 4 + z_lo), core: 2. Of those that a mesh axis runs over, the one named last changes fastest.
Arguments:
- candidates: bfloat16 [49152, 1024], P(('pages', 'heads')), may hold values from -6 to 6
- in_weight: bfloat16 [2, 1024, 8, 512], P(None, None, 'heads'), may hold values from -0.1875 to 0.1875
- out_weight: bfloat16 [2, 8, 128, 1024], P(None, 'heads'), may hold values from -0.1875 to 0.1875
- page_cache: bfloat16 [2, 4096, 8, 2, 32, 128], P(None, 'pages', 'heads'), may hold values from -6 to 6
- page_lists: int32 [1024, 4], P('pages'), may hold values from 0 to 4095, as said below
- hist_len: int32 [1024], P('pages'), may hold values from 1 to 128
Outputs:
- hidden_out: bfloat16 [49152, 1024], P(('pages', 'heads'))
Inputs may be any that keep to these rules, and one draw needn't show every extreme that they name: `page_lists`: every page id appears in exactly one list. Page p lies on index p // 64 of pages; the requests of one index of pages list either none or exactly 2 pages that lie on any one index.
All inputs are finite; a program needn't handle non-finite values.
Results may differ from a plain program's by a relative error of at most 0.018.
Values may be sent and summed in bfloat16 or wider, within the bound.
A program may use at most 64 MiB of HBM per device.

v0:
```python
import math
import jax
import jax.numpy as jnp
from jax import lax
from jax.sharding import PartitionSpec as P

eps = 1e-05


def layer_norm(values):
    row_mean = jnp.mean(values, -1, keepdims=True)
    centred = values - row_mean
    spread = jnp.mean(centred * centred, -1, keepdims=True)
    return centred * lax.rsqrt(spread + eps)


def on_device(candidates, in_weight, out_weight, page_cache, page_lists, hist_len):
    readers = lax.axis_size("pages")
    head_group = lax.axis_size("heads")
    layers = in_weight.shape[0]
    model_width = in_weight.shape[1]
    heads_here = in_weight.shape[2]
    head_dim = out_weight.shape[2]
    pages_here = page_cache.shape[1]
    page_len = page_cache.shape[4]
    requests, max_pages = page_lists.shape
    slot_count = requests * max_pages
    capacity = 2 * slot_count // readers
    shard_rows = candidates.shape[0]
    cand_rows = shard_rows * head_group
    per_request = cand_rows // requests
    score_scale = 1.0 / math.sqrt(head_dim)
    flat_ids = page_lists.reshape(slot_count)
    slot_owner = flat_ids // pages_here
    local_ids = flat_ids % pages_here
    slot_order = jnp.arange(slot_count)
    earlier_same = (slot_owner[None, :] == slot_owner[:, None]) & (
        slot_order[None, :] < slot_order[:, None]
    )
    slot_rank = jnp.sum(earlier_same.astype(jnp.int32), axis=1)
    places = slot_owner * capacity + slot_rank
    divisors = (hist_len + 1).astype(jnp.float32)
    cand_divisors = jnp.repeat(divisors, per_request)
    slot_targets = jnp.arange(readers * capacity)
    matches = places[None, :] == slot_targets[:, None]
    filled = jnp.any(matches, axis=1)
    inverse = jnp.sum(jnp.where(matches, slot_order[None, :], 0), axis=1)
    asked_request = inverse // max_pages
    page_of_slot = slot_order % max_pages
    valid_tokens = jnp.clip(jnp.repeat(hist_len, max_pages) - page_of_slot * page_len, 0, page_len)
    slot_meta = jnp.stack(
        [
            jnp.take(local_ids, inverse),
            jnp.take(valid_tokens, inverse),
            jnp.take(hist_len, asked_request),
        ],
        axis=-1,
    )
    slot_meta = jnp.where(filled[:, None], slot_meta, 0).reshape(readers, capacity, 3)
    hidden_rows = candidates
    for layer_index in range(layers):
        weights_in = in_weight[layer_index].reshape(model_width, heads_here * 4 * head_dim)
        ready = layer_norm(
            lax.all_gather(hidden_rows, "heads", axis=0, tiled=True).astype(jnp.float32)
        ).astype(jnp.bfloat16)
        projected = jax.nn.silu(jnp.dot(ready, weights_in, preferred_element_type=jnp.float32))
        projected = projected.reshape(cand_rows, heads_here, 4 * head_dim)
        gate_part = projected[:, :, :head_dim]
        value_part = projected[:, :, head_dim : 2 * head_dim].astype(jnp.bfloat16)
        query_part = projected[:, :, 2 * head_dim : 3 * head_dim].astype(jnp.bfloat16)
        key_part = projected[:, :, 3 * head_dim :].astype(jnp.bfloat16)
        queries = query_part.reshape(requests, per_request, heads_here, head_dim)
        sent_queries = jnp.take(queries, asked_request, axis=0)
        sent_queries = jnp.where(
            filled[:, None, None, None], sent_queries, jnp.zeros((), jnp.bfloat16)
        )
        sent_queries = sent_queries.reshape(readers, capacity, per_request, heads_here, head_dim)
        got_queries, got_meta = (
            lax.all_to_all(sent_queries, "pages", split_axis=0, concat_axis=0, tiled=True),
            lax.all_to_all(slot_meta, "pages", split_axis=0, concat_axis=0, tiled=True),
        )
        page_rows = jnp.take(
            page_cache[layer_index], got_meta[:, :, 0].reshape(readers * capacity), axis=0
        )
        page_rows = page_rows.reshape(readers, capacity, heads_here, 2, page_len, head_dim)
        scores = (
            jnp.einsum(
                "ncqhd,nchtd->nchqt",
                got_queries,
                page_rows[:, :, :, 0],
                preferred_element_type=jnp.float32,
            )
            * score_scale
        )
        keep_mask = jnp.arange(page_len)[None, None, :] < got_meta[:, :, 1][:, :, None]
        owner_divisors = (got_meta[:, :, 2] + 1).astype(jnp.float32)
        weights = (
            jnp.where(keep_mask[:, :, None, None, :], jax.nn.silu(scores), 0.0)
            / owner_divisors[:, :, None, None, None]
        )
        weights = weights.astype(jnp.bfloat16)
        partial_out = jnp.einsum(
            "nchqt,nchtd->ncqhd", weights, page_rows[:, :, :, 1], preferred_element_type=jnp.float32
        )
        returned = lax.all_to_all(
            partial_out.astype(jnp.bfloat16), "pages", split_axis=0, concat_axis=0, tiled=True
        ).astype(partial_out.dtype)
        returned_rows = jnp.take(
            returned.reshape(readers * capacity, per_request, heads_here, head_dim), places, axis=0
        )
        attended_hist = jnp.sum(
            returned_rows.reshape(requests, max_pages, per_request, heads_here, head_dim), axis=1
        )
        attended = attended_hist.reshape(cand_rows, heads_here, head_dim)
        self_score = (
            jnp.sum(query_part.astype(jnp.float32) * key_part.astype(jnp.float32), -1) * score_scale
        )
        self_weight = (jax.nn.silu(self_score) / cand_divisors[:, None]).astype(jnp.bfloat16)
        attended = attended + self_weight.astype(jnp.float32)[:, :, None] * value_part.astype(
            jnp.float32
        )
        gated_rows = (
            (layer_norm(attended) * gate_part)
            .astype(jnp.bfloat16)
            .reshape(cand_rows, heads_here * head_dim)
        )
        weights_out = out_weight[layer_index].reshape(heads_here * head_dim, model_width)
        summed = lax.psum_scatter(
            jnp.dot(gated_rows, weights_out, preferred_element_type=jnp.float32).astype(
                jnp.bfloat16
            ),
            "heads",
            scatter_dimension=0,
            tiled=True,
        ).astype(jnp.float32)
        hidden_rows = (hidden_rows.astype(jnp.float32) + summed).astype(jnp.bfloat16)
    return hidden_rows


def solution(mesh):
    in_specs = (
        P(("pages", "heads"), None),
        P(None, None, "heads", None),
        P(None, "heads", None, None),
        P(None, "pages", "heads", None, None, None),
        P("pages", None),
        P("pages"),
    )
    out_specs = P(("pages", "heads"), None)
    return jax.shard_map(
        on_device, mesh=mesh, in_specs=in_specs, out_specs=out_specs, check_vma=False
    )
```

profile of v0, /device:TPU:8, one launch (start us, length us, event | category | flops | bytes accessed | tf_op | source)
XLA Modules:
  0.0 597.3 jit_solution(8234759997289166943)
XLA Ops:
  13.8 10.1 %broadcast_select_fusion.1 = (s32[128]{0:T(128)S(1)}, s32[128]{0:T(128)S(1)}, s32[128]{0:T(128)S(1)}) fusion(s32[128]{0:T(128)S(1)} %gather_fusion, s32[128]{0:T(128)S(1)} %select_reduce_fusion, s32[128]{0:T(128)S(1)} %gather_fusion.1, s32[]{:T(128)} %bitcast.25, s32[]{:T(128)} %bitcast.24, s32[]{:T(128)} %bitcast.23, s32[]{:T(128)} %bitcast.22, ...), kind=kLoop, calls=%fused_computation.158 | loop fusion | flops 7168 | bytes 3136 | tf_op jit(solution)/shard_map/jit(_take)/select_n | solution.py:53
  25.8 13.5 %all-to-all-start = ((s32[64,2,3]{2,1,0:T(2,128)}), s32[64,2,3]{2,1,0:T(2,128)S(1)}, u32[]{:S(2)}, u32[]{:S(2)}) async-start(s32[64,2,3]{2,1,0:T(2,128)} %copy.62), calls=%async_computation | async-start | bytes 131072 | tf_op jit(solution)/shard_map/all_to_all | solution.py:80
  39.4 50.6 %all-gather.3.cloned.1.call-done = bf16[768,1024]{1,0:T(8,128)(2,1)} async-done(((bf16[96,1024]{1,0:T(8,128)(2,1)}), bf16[768,1024]{1,0:T(8,128)(2,1)}) %all-gather.3.cloned.1.call-update) | async-done | bytes 1572880 | tf_op jit(solution)/shard_map/all_gather | solution.py:64
  92.5 3.7 fusion.70
  98.7 8.5 %all-to-all-start.1 = ((bf16[64,2,48,1,128]{4,2,1,3,0:T(8,128)(2,1)}), bf16[64,2,48,1,128]{4,2,1,3,0:T(8,128)(2,1)}, u32[]{:S(2)}, u32[]{:S(2)}) async-start(bf16[64,2,48,1,128]{4,2,1,3,0:T(8,128)(2,1)} %bitcast.38), calls=%async_computation.1 | async-start | bytes 3145728 | tf_op jit(solution)/shard_map/all_to_all | solution.py:79
  119.8 26.4 %all-to-all-done.1 = bf16[64,2,48,1,128]{4,2,1,3,0:T(8,128)(2,1)} async-done(((bf16[64,2,48,1,128]{4,2,1,3,0:T(8,128)(2,1)}), bf16[64,2,48,1,128]{4,2,1,3,0:T(8,128)(2,1)}, u32[]{:S(2)}, u32[]{:S(2)}) %all-to-all-start.1) | async-done | bytes 1572896 | tf_op jit(solution)/shard_map/all_to_all | solution.py:79
  146.3 4.0 fusion.20
  150.3 6.9 %all-to-all-start.2 = ((bf16[64,2,48,1,128]{4,2,1,3,0:T(8,128)(2,1)}), bf16[64,2,48,1,128]{4,2,1,3,0:T(8,128)(2,1)}, u32[]{:S(2)}, u32[]{:S(2)}) async-start(bf16[64,2,48,1,128]{4,2,1,3,0:T(8,128)(2,1)} %fusion.20), calls=%async_computation.2 | async-start | bytes 3145728 | tf_op jit(solution)/shard_map/all_to_all | solution.py:105
  157.8 38.5 %all-to-all-done.2 = bf16[64,2,48,1,128]{4,2,1,3,0:T(8,128)(2,1)} async-done(((bf16[64,2,48,1,128]{4,2,1,3,0:T(8,128)(2,1)}), bf16[64,2,48,1,128]{4,2,1,3,0:T(8,128)(2,1)}, u32[]{:S(2)}, u32[]{:S(2)}) %all-to-all-start.2) | async-done | bytes 1572896 | tf_op jit(solution)/shard_map/all_to_all | solution.py:105
  196.2 3.3 bitcast_convert_fusion.1
  199.6 3.7 gather_fusion.4
  203.3 2.8 bitcast_select_fusion.4
  208.6 2.8 convolution_convert_fusion.3
  211.5 92.5 %reduce-scatter.3.cloned.1.call-done = bf16[96,1024]{1,0:T(8,128)(2,1)} async-done(((bf16[768,1024]{1,0:T(8,128)(2,1)}), bf16[96,1024]{1,0:T(8,128)(2,1)}) %reduce-scatter.3.cloned.1.call-update) | async-done | bytes 196624 | tf_op jit(solution)/shard_map/reduce_scatter | solution.py:128
  305.8 71.9 %all-gather.5.cloned.1.call-done = bf16[768,1024]{1,0:T(8,128)(2,1)} async-done(((bf16[96,1024]{1,0:T(8,128)(2,1)}), bf16[768,1024]{1,0:T(8,128)(2,1)}) %all-gather.5.cloned.1.call-update) | async-done | bytes 1572880 | tf_op jit(solution)/shard_map/all_gather | solution.py:64
  380.1 3.6 fusion.71
  385.7 2.7 fusion.13
  388.4 8.5 %all-to-all-start.3 = ((bf16[64,2,48,1,128]{4,2,1,3,0:T(8,128)(2,1)}), bf16[64,2,48,1,128]{4,2,1,3,0:T(8,128)(2,1)}, u32[]{:S(2)}, u32[]{:S(2)}) async-start(bf16[64,2,48,1,128]{4,2,1,3,0:T(8,128)(2,1)} %bitcast.191), calls=%async_computation.4 | async-start | bytes 3145728 | tf_op jit(solution)/shard_map/all_to_all | solution.py:79
  398.7 37.3 %all-to-all-done.3 = bf16[64,2,48,1,128]{4,2,1,3,0:T(8,128)(2,1)} async-done(((bf16[64,2,48,1,128]{4,2,1,3,0:T(8,128)(2,1)}), bf16[64,2,48,1,128]{4,2,1,3,0:T(8,128)(2,1)}, u32[]{:S(2)}, u32[]{:S(2)}) %all-to-all-start.3) | async-done | bytes 1572896 | tf_op jit(solution)/shard_map/all_to_all | solution.py:79
  436.0 4.0 fusion.21
  440.0 6.6 %all-to-all-start.4 = ((bf16[64,2,48,1,128]{4,2,1,3,0:T(8,128)(2,1)}), bf16[64,2,48,1,128]{4,2,1,3,0:T(8,128)(2,1)S(1)}, u32[]{:S(2)}, u32[]{:S(2)}) async-start(bf16[64,2,48,1,128]{4,2,1,3,0:T(8,128)(2,1)} %fusion.21), calls=%async_computation.5 | async-start | bytes 3145728 | tf_op jit(solution)/shard_map/all_to_all | solution.py:105
  446.9 38.9 %all-to-all-done.4 = bf16[64,2,48,1,128]{4,2,1,3,0:T(8,128)(2,1)S(1)} async-done(((bf16[64,2,48,1,128]{4,2,1,3,0:T(8,128)(2,1)}), bf16[64,2,48,1,128]{4,2,1,3,0:T(8,128)(2,1)S(1)}, u32[]{:S(2)}, u32[]{:S(2)}) %all-to-all-start.4) | async-done | bytes 1572896 | tf_op jit(solution)/shard_map/all_to_all | solution.py:105
  493.9 2.8 convolution_convert_fusion.2
  496.7 92.4 %reduce-scatter.5.cloned.1.call-done = bf16[96,1024]{1,0:T(8,128)(2,1)} async-done(((bf16[768,1024]{1,0:T(8,128)(2,1)}), bf16[96,1024]{1,0:T(8,128)(2,1)}) %reduce-scatter.5.cloned.1.call-update) | async-done | bytes 196624 | tf_op jit(solution)/shard_map/reduce_scatter | solution.py:128
  (107 shorter events, 47.6 us)
Async XLA Ops:
  6.5 83.5 %all-gather.3.cloned.1.call-start = ((), (), s32[]{:S(2)}) async-start(), calls=%async_computation.7 | async-start | bytes 1769472 | tf_op jit(solution)/shard_map/all_gather | solution.py:64
  25.8 72.8 %all-to-all-start = ((s32[64,2,3]{2,1,0:T(2,128)}), s32[64,2,3]{2,1,0:T(2,128)S(1)}, u32[]{:S(2)}, u32[]{:S(2)}) async-start(s32[64,2,3]{2,1,0:T(2,128)} %copy.62), calls=%async_computation | async-start | bytes 131072 | tf_op jit(solution)/shard_map/all_to_all | solution.py:80
  90.1 1.9 copy-start
  98.7 47.6 %all-to-all-start.1 = ((bf16[64,2,48,1,128]{4,2,1,3,0:T(8,128)(2,1)}), bf16[64,2,48,1,128]{4,2,1,3,0:T(8,128)(2,1)}, u32[]{:S(2)}, u32[]{:S(2)}) async-start(bf16[64,2,48,1,128]{4,2,1,3,0:T(8,128)(2,1)} %bitcast.38), calls=%async_computation.1 | async-start | bytes 3145728 | tf_op jit(solution)/shard_map/all_to_all | solution.py:79
  150.3 7.1 %copy-start.6 = (s32[16]{0:T(128)S(1)}, s32[16]{0:T(128)}, u32[]{:S(2)}) copy-start(s32[16]{0:T(128)} %param.19) | copy-start | bytes 196
  150.3 46.0 %all-to-all-start.2 = ((bf16[64,2,48,1,128]{4,2,1,3,0:T(8,128)(2,1)}), bf16[64,2,48,1,128]{4,2,1,3,0:T(8,128)(2,1)}, u32[]{:S(2)}, u32[]{:S(2)}) async-start(bf16[64,2,48,1,128]{4,2,1,3,0:T(8,128)(2,1)} %fusion.20), calls=%async_computation.2 | async-start | bytes 3145728 | tf_op jit(solution)/shard_map/all_to_all | solution.py:105
  157.2 146.9 %reduce-scatter.3.cloned.1.call-start = ((), (), s32[]{:S(2)}) async-start(), calls=%async_computation.8 | async-start | bytes 1769472 | tf_op jit(solution)/shard_map/reduce_scatter | solution.py:128
  207.6 1.0 copy-start.4
  208.6 95.4 %copy-start.3 = (bf16[96,1024]{1,0:T(8,128)(2,1)S(1)}, bf16[96,1024]{1,0:T(8,128)(2,1)}, u32[]{:S(2)}) copy-start(bf16[96,1024]{1,0:T(8,128)(2,1)} %param.14) | copy-start | bytes 589828
  211.5 166.2 %all-gather.5.cloned.1.call-start = ((), (), s32[]{:S(2)}) async-start(), calls=%async_computation.9 | async-start | bytes 1769472 | tf_op jit(solution)/shard_map/all_gather | solution.py:64
  377.7 1.9 copy-start.1
  388.4 47.6 %all-to-all-start.3 = ((bf16[64,2,48,1,128]{4,2,1,3,0:T(8,128)(2,1)}), bf16[64,2,48,1,128]{4,2,1,3,0:T(8,128)(2,1)}, u32[]{:S(2)}, u32[]{:S(2)}) async-start(bf16[64,2,48,1,128]{4,2,1,3,0:T(8,128)(2,1)} %bitcast.191), calls=%async_computation.4 | async-start | bytes 3145728 | tf_op jit(solution)/shard_map/all_to_all | solution.py:79
  440.0 45.7 %all-to-all-start.4 = ((bf16[64,2,48,1,128]{4,2,1,3,0:T(8,128)(2,1)}), bf16[64,2,48,1,128]{4,2,1,3,0:T(8,128)(2,1)S(1)}, u32[]{:S(2)}, u32[]{:S(2)}) async-start(bf16[64,2,48,1,128]{4,2,1,3,0:T(8,128)(2,1)} %fusion.21), calls=%async_computation.5 | async-start | bytes 3145728 | tf_op jit(solution)/shard_map/all_to_all | solution.py:105
  446.6 142.5 %reduce-scatter.5.cloned.1.call-start = ((), (), s32[]{:S(2)}) async-start(), calls=%async_computation.10 | async-start | bytes 1769472 | tf_op jit(solution)/shard_map/reduce_scatter | solution.py:128
  491.6 2.2 copy-start.5
  493.9 95.2 %copy-start.2 = (bf16[96,1024]{1,0:T(8,128)(2,1)S(1)}, bf16[96,1024]{1,0:T(8,128)(2,1)}, u32[]{:S(2)}) copy-start(bf16[96,1024]{1,0:T(8,128)(2,1)} %add_convert_fusion.1) | copy-start | bytes 589828
Sparse Core Ops, SparseCore 0:
  10.5 79.5 all-gather.2
  211.6 92.4 reduce-scatter.2
  307.3 70.3 all-gather.4
  496.8 92.2 reduce-scatter.4
where the time goes:
time: 599 us; the launch traced here: 597 us
  waiting for transfers between devices  449 us (75%)
  starting transfers between devices  44.3 us (7%)
  other arithmetic  39.9 us (7%)
  local copies, waits for them, and re-layouts  29.2 us (5%)
  matrix products  20.9 us (3%)
  between operations  13.5 us (2%)
    reduce_scatter x2, waiting for transfers between devices, on_device(): lax.psum_scatter(jnp.dot(gated_rows, weights_out, preferred_element_type=...  185 us
    all_gather x2, waiting for transfers between devices, on_device(): lax.all_gather(hidden_rows, 'heads', axis=0, tiled=True).astype(jnp.float32)  123 us
    all_to_all x2, waiting for transfers between devices, on_device(): lax.all_to_all(partial_out.astype(jnp.bfloat16), 'pages', split_axis=0, c...  77.4 us
    all_to_all x2, waiting for transfers between devices, on_device(): lax.all_to_all(sent_queries, 'pages', split_axis=0, concat_axis=0, tiled=...  63.8 us
    all_to_all x2, starting transfers between devices, on_device(): lax.all_to_all(sent_queries, 'pages', split_axis=0, concat_axis=0, tiled=...  17 us
    all_to_all x1, starting transfers between devices, on_device(): lax.all_to_all(slot_meta, 'pages', split_axis=0, concat_axis=0, tiled=True)  13.5 us
    all_to_all x2, starting transfers between devices, on_device(): lax.all_to_all(partial_out.astype(jnp.bfloat16), 'pages', split_axis=0, c...  13.5 us
  transfers between devices with their start and end apart: 9, of which 8 were waited for; matrix products, arithmetic and copies ran while one was open for 7% of the time, Pallas kernels for 0%

commit v1 on v0

--- a/solution.py
+++ b/solution.py
@@ -61,7 +61,12 @@
     for layer_index in range(layers):
         weights_in = in_weight[layer_index].reshape(model_width, heads_here * 4 * head_dim)
         ready = layer_norm(
-            lax.all_gather(hidden_rows, "heads", axis=0, tiled=True).astype(jnp.float32)
+            jnp.concatenate(
+                lax.all_to_all(
+                    jnp.stack([hidden_rows for _ in range(lax.axis_size("heads"))]), "heads", 0, 0
+                ),
+                axis=0,
+            ).astype(jnp.float32)
         ).astype(jnp.bfloat16)
         projected = jax.nn.silu(jnp.dot(ready, weights_in, preferred_element_type=jnp.float32))
         projected = projected.reshape(cand_rows, heads_here, 4 * head_dim)

time: 599 us -> 550 us (0.918)
  waiting for transfers between devices: 449 us -> 334 us
  starting transfers between devices: 44.3 us -> 88.4 us
  blocking collectives: 0 us -> 26.8 us
    all_gather x2 -> x0, waiting for transfers between devices: 123 us -> none  [on_device(): lax.all_gather(hidden_rows, 'heads', axis=0, tiled=True).astype(jnp.float32)]
    all_to_all x0 -> x1, blocking collectives: none -> 26.8 us  [on_device(): lax.all_to_all(jnp.stack([hidden_rows for _ in range(lax.axis_size('heads...]
    all_to_all x2, starting transfers between devices: 17 us -> 35.2 us  [on_device(): lax.all_to_all(sent_queries, 'pages', split_axis=0, concat_axis=0, tiled=...]
    all_to_all x1, starting transfers between devices: 13.5 us -> 26.5 us  [on_device(): lax.all_to_all(slot_meta, 'pages', split_axis=0, concat_axis=0, tiled=True)]
    all_to_all x0 -> x1, starting transfers between devices: none -> 12.9 us  [on_device(): lax.all_to_all(jnp.stack([hidden_rows for _ in range(lax.axis_size('heads...]
    all_to_all x0 -> x1, waiting for transfers between devices: none -> 9.39 us  [on_device(): lax.all_to_all(jnp.stack([hidden_rows for _ in range(lax.axis_size('heads...]
  transfers between devices with their start and end apart: 9 -> 8, of which waited for: 8 -> 8; matrix products, arithmetic and copies ran while one was open for 7% -> 7% of each run, Pallas kernels for 0% -> 0%
where the time goes in v1:
time: 550 us; the launch traced here: 548 us
  waiting for transfers between devices  334 us (61%)
  starting transfers between devices  88.4 us (16%)
  other arithmetic  36.5 us (7%)
  local copies, waits for them, and re-layouts  30.6 us (6%)
  blocking collectives  26.8 us (5%)
  matrix products  18.3 us (3%)
  between operations  13.9 us (3%)
    reduce_scatter x2, waiting for transfers between devices, on_device(): lax.psum_scatter(jnp.dot(gated_rows, weights_out, preferred_element_type=...  181 us
    all_to_all x2, waiting for transfers between devices, on_device(): lax.all_to_all(partial_out.astype(jnp.bfloat16), 'pages', split_axis=0, c...  77.3 us
    all_to_all x2, waiting for transfers between devices, on_device(): lax.all_to_all(sent_queries, 'pages', split_axis=0, concat_axis=0, tiled=...  63.8 us
    all_to_all x2, starting transfers between devices, on_device(): lax.all_to_all(sent_queries, 'pages', split_axis=0, concat_axis=0, tiled=...  35.2 us
    all_to_all x1, blocking collectives, on_device(): lax.all_to_all(jnp.stack([hidden_rows for _ in range(lax.axis_size('heads...  26.8 us
    all_to_all x1, starting transfers between devices, on_device(): lax.all_to_all(slot_meta, 'pages', split_axis=0, concat_axis=0, tiled=True)  26.5 us
    all_to_all x2, starting transfers between devices, on_device(): lax.all_to_all(partial_out.astype(jnp.bfloat16), 'pages', split_axis=0, c...  13.5 us
    all_to_all x1, starting transfers between devices, on_device(): lax.all_to_all(jnp.stack([hidden_rows for _ in range(lax.axis_size('heads...  12.9 us
  transfers between devices with their start and end apart: 8, of which 8 were waited for; matrix products, arithmetic and copies ran while one was open for 7% of the time, Pallas kernels for 0%

profile of v1, /device:TPU:8, one launch (start us, length us, event | category | flops | bytes accessed | tf_op | source)
XLA Modules:
  0.0 548.4 jit_solution(3523454597380380697)
XLA Ops:
  8.8 12.9 %all-to-all-start.1 = ((bf16[8,96,1024]{2,1,0:T(8,128)(2,1)}), bf16[8,96,1024]{2,1,0:T(8,128)(2,1)S(1)}, u32[]{:S(2)}, u32[]{:S(2)}) async-start(bf16[8,96,1024]{2,1,0:T(8,128)(2,1)} %stack.13), calls=%async_computation.1 | async-start | bytes 3145728 | tf_op jit(solution)/shard_map/all_to_all | solution.py:65
  25.7 10.1 %broadcast_select_fusion.1 = (s32[128]{0:T(128)S(1)}, s32[128]{0:T(128)S(1)}, s32[128]{0:T(128)S(1)}) fusion(s32[128]{0:T(128)S(1)} %gather_fusion, s32[128]{0:T(128)S(1)} %select_reduce_fusion, s32[128]{0:T(128)S(1)} %gather_fusion.1, s32[]{:T(128)} %bitcast.25, s32[]{:T(128)} %bitcast.24, s32[]{:T(128)} %bitcast.23, s32[]{:T(128)} %bitcast.22, ...), kind=kLoop, calls=%fused_computation.154 | loop fusion | flops 7168 | bytes 3136 | tf_op jit(solution)/shard_map/jit(_take)/select_n | solution.py:53
  37.8 9.4 %all-to-all-done.1 = bf16[8,96,1024]{2,1,0:T(8,128)(2,1)S(1)} async-done(((bf16[8,96,1024]{2,1,0:T(8,128)(2,1)}), bf16[8,96,1024]{2,1,0:T(8,128)(2,1)S(1)}, u32[]{:S(2)}, u32[]{:S(2)}) %all-to-all-start.1) | async-done | bytes 1572896 | tf_op jit(solution)/shard_map/all_to_all | solution.py:65
  47.1 26.5 %all-to-all-start = ((s32[64,2,3]{2,1,0:T(2,128)}), s32[64,2,3]{2,1,0:T(2,128)S(1)}, u32[]{:S(2)}, u32[]{:S(2)}) async-start(s32[64,2,3]{2,1,0:T(2,128)} %copy.62), calls=%async_computation | async-start | bytes 131072 | tf_op jit(solution)/shard_map/all_to_all | solution.py:85
  83.0 8.8 %all-to-all-start.2 = ((bf16[64,2,48,1,128]{4,2,1,3,0:T(8,128)(2,1)}), bf16[64,2,48,1,128]{4,2,1,3,0:T(8,128)(2,1)}, u32[]{:S(2)}, u32[]{:S(2)}) async-start(bf16[64,2,48,1,128]{4,2,1,3,0:T(8,128)(2,1)} %bitcast.39), calls=%async_computation.2 | async-start | bytes 3145728 | tf_op jit(solution)/shard_map/all_to_all | solution.py:84
  99.6 2.7 bitcast_select_fusion
  104.5 26.4 %all-to-all-done.2 = bf16[64,2,48,1,128]{4,2,1,3,0:T(8,128)(2,1)} async-done(((bf16[64,2,48,1,128]{4,2,1,3,0:T(8,128)(2,1)}), bf16[64,2,48,1,128]{4,2,1,3,0:T(8,128)(2,1)}, u32[]{:S(2)}, u32[]{:S(2)}) %all-to-all-start.2) | async-done | bytes 1572896 | tf_op jit(solution)/shard_map/all_to_all | solution.py:84
  130.9 4.0 fusion.12
  134.9 6.8 %all-to-all-start.3 = ((bf16[64,2,48,1,128]{4,2,1,3,0:T(8,128)(2,1)}), bf16[64,2,48,1,128]{4,2,1,3,0:T(8,128)(2,1)}, u32[]{:S(2)}, u32[]{:S(2)}) async-start(bf16[64,2,48,1,128]{4,2,1,3,0:T(8,128)(2,1)} %fusion.12), calls=%async_computation.3 | async-start | bytes 3145728 | tf_op jit(solution)/shard_map/all_to_all | solution.py:110
  142.3 38.5 %all-to-all-done.3 = bf16[64,2,48,1,128]{4,2,1,3,0:T(8,128)(2,1)} async-done(((bf16[64,2,48,1,128]{4,2,1,3,0:T(8,128)(2,1)}), bf16[64,2,48,1,128]{4,2,1,3,0:T(8,128)(2,1)}, u32[]{:S(2)}, u32[]{:S(2)}) %all-to-all-start.3) | async-done | bytes 1572896 | tf_op jit(solution)/shard_map/all_to_all | solution.py:110
  180.8 3.3 bitcast_convert_fusion.1
  184.1 3.7 gather_fusion.4
  187.8 2.8 bitcast_select_fusion.4
  193.2 2.8 convolution_convert_fusion.3
  196.0 91.0 %reduce-scatter.3.cloned.1.call-done = bf16[96,1024]{1,0:T(8,128)(2,1)} async-done(((bf16[768,1024]{1,0:T(8,128)(2,1)}), bf16[96,1024]{1,0:T(8,128)(2,1)}) %reduce-scatter.3.cloned.1.call-update) | async-done | bytes 196624 | tf_op jit(solution)/shard_map/reduce_scatter | solution.py:133
  288.2 26.8 %all_to_all.36 = bf16[8,96,1024]{2,1,0:T(8,128)(2,1)S(1)} all-to-all(bf16[8,96,1024]{2,1,0:T(8,128)(2,1)S(1)} %stack.14), channel_id=1, replica_groups=mesh['pages'=64,'heads'=8] {'heads'}, dimensions={0} | all-to-all | bytes 3145728 | tf_op jit(solution)/shard_map/all_to_all | solution.py:65
  321.8 2.8 fusion.9
  324.6 26.4 %all-to-all-start.5 = ((bf16[64,2,48,1,128]{4,2,1,3,0:T(8,128)(2,1)}), bf16[64,2,48,1,128]{4,2,1,3,0:T(8,128)(2,1)}, u32[]{:S(2)}, u32[]{:S(2)}) async-start(bf16[64,2,48,1,128]{4,2,1,3,0:T(8,128)(2,1)} %bitcast.195), calls=%async_computation.6 | async-start | bytes 3145728 | tf_op jit(solution)/shard_map/all_to_all | solution.py:84
  352.7 37.3 %all-to-all-done.5 = bf16[64,2,48,1,128]{4,2,1,3,0:T(8,128)(2,1)} async-done(((bf16[64,2,48,1,128]{4,2,1,3,0:T(8,128)(2,1)}), bf16[64,2,48,1,128]{4,2,1,3,0:T(8,128)(2,1)}, u32[]{:S(2)}, u32[]{:S(2)}) %all-to-all-start.5) | async-done | bytes 1572896 | tf_op jit(solution)/shard_map/all_to_all | solution.py:84
  390.1 4.0 fusion.13
  394.1 6.8 %all-to-all-start.6 = ((bf16[64,2,48,1,128]{4,2,1,3,0:T(8,128)(2,1)}), bf16[64,2,48,1,128]{4,2,1,3,0:T(8,128)(2,1)}, u32[]{:S(2)}, u32[]{:S(2)}) async-start(bf16[64,2,48,1,128]{4,2,1,3,0:T(8,128)(2,1)} %fusion.13), calls=%async_computation.7 | async-start | bytes 3145728 | tf_op jit(solution)/shard_map/all_to_all | solution.py:110
  401.1 38.8 %all-to-all-done.6 = bf16[64,2,48,1,128]{4,2,1,3,0:T(8,128)(2,1)} async-done(((bf16[64,2,48,1,128]{4,2,1,3,0:T(8,128)(2,1)}), bf16[64,2,48,1,128]{4,2,1,3,0:T(8,128)(2,1)}, u32[]{:S(2)}, u32[]{:S(2)}) %all-to-all-start.6) | async-done | bytes 1572896 | tf_op jit(solution)/shard_map/all_to_all | solution.py:110
  446.7 2.8 convolution_convert_fusion.2
  449.5 90.4 %reduce-scatter.5.cloned.1.call-done = bf16[96,1024]{1,0:T(8,128)(2,1)} async-done(((bf16[768,1024]{1,0:T(8,128)(2,1)}), bf16[96,1024]{1,0:T(8,128)(2,1)}) %reduce-scatter.5.cloned.1.call-update) | async-done | bytes 196624 | tf_op jit(solution)/shard_map/reduce_scatter | solution.py:133
  (110 shorter events, 48.7 us)
Async XLA Ops:
  8.8 12.9 %copy-start.5 = (s32[16,4]{0,1:T(4,128)S(1)}, s32[16,4]{0,1:T(4,128)}, u32[]{:S(2)}) copy-start(s32[16,4]{0,1:T(4,128)} %param.18) | copy-start | bytes 772
  8.8 13.1 %copy-start.4 = (s32[16]{0:T(128)S(1)}, s32[16]{0:T(128)}, u32[]{:S(2)}) copy-start(s32[16]{0:T(128)} %param.19) | copy-start | bytes 196
  8.8 38.3 %all-to-all-start.1 = ((bf16[8,96,1024]{2,1,0:T(8,128)(2,1)}), bf16[8,96,1024]{2,1,0:T(8,128)(2,1)S(1)}, u32[]{:S(2)}, u32[]{:S(2)}) async-start(bf16[8,96,1024]{2,1,0:T(8,128)(2,1)} %stack.13), calls=%async_computation.1 | async-start | bytes 3145728 | tf_op jit(solution)/shard_map/all_to_all | solution.py:65
  47.1 35.8 %all-to-all-start = ((s32[64,2,3]{2,1,0:T(2,128)}), s32[64,2,3]{2,1,0:T(2,128)S(1)}, u32[]{:S(2)}, u32[]{:S(2)}) async-start(s32[64,2,3]{2,1,0:T(2,128)} %copy.62), calls=%async_computation | async-start | bytes 131072 | tf_op jit(solution)/shard_map/all_to_all | solution.py:85
  74.6 1.6 copy-start.6
  83.0 47.9 %all-to-all-start.2 = ((bf16[64,2,48,1,128]{4,2,1,3,0:T(8,128)(2,1)}), bf16[64,2,48,1,128]{4,2,1,3,0:T(8,128)(2,1)}, u32[]{:S(2)}, u32[]{:S(2)}) async-start(bf16[64,2,48,1,128]{4,2,1,3,0:T(8,128)(2,1)} %bitcast.39), calls=%async_computation.2 | async-start | bytes 3145728 | tf_op jit(solution)/shard_map/all_to_all | solution.py:84
  134.9 45.9 %all-to-all-start.3 = ((bf16[64,2,48,1,128]{4,2,1,3,0:T(8,128)(2,1)}), bf16[64,2,48,1,128]{4,2,1,3,0:T(8,128)(2,1)}, u32[]{:S(2)}, u32[]{:S(2)}) async-start(bf16[64,2,48,1,128]{4,2,1,3,0:T(8,128)(2,1)} %fusion.12), calls=%async_computation.3 | async-start | bytes 3145728 | tf_op jit(solution)/shard_map/all_to_all | solution.py:110
  141.7 145.3 %reduce-scatter.3.cloned.1.call-start = ((), (), s32[]{:S(2)}) async-start(), calls=%async_computation.9 | async-start | bytes 1769472 | tf_op jit(solution)/shard_map/reduce_scatter | solution.py:133
  192.1 1.0 copy-start.2
  193.2 93.8 %copy-start = (bf16[96,1024]{1,0:T(8,128)(2,1)S(1)}, bf16[96,1024]{1,0:T(8,128)(2,1)}, u32[]{:S(2)}) copy-start(bf16[96,1024]{1,0:T(8,128)(2,1)} %param.14) | copy-start | bytes 589828
  315.9 1.6 copy-start.7
  319.8 81.1 %copy-start.1 = (bf16[768,1,512]{2,0,1:T(8,128)(2,1)}, bf16[768,1,512]{2,0,1:T(8,128)(2,1)S(1)}, u32[]{:S(2)}) copy-start(bf16[768,1,512]{2,0,1:T(8,128)(2,1)S(1)} %get-tuple-element.47) | copy-start | bytes 2359300
  324.6 65.5 %all-to-all-start.5 = ((bf16[64,2,48,1,128]{4,2,1,3,0:T(8,128)(2,1)}), bf16[64,2,48,1,128]{4,2,1,3,0:T(8,128)(2,1)}, u32[]{:S(2)}, u32[]{:S(2)}) async-start(bf16[64,2,48,1,128]{4,2,1,3,0:T(8,128)(2,1)} %bitcast.195), calls=%async_computation.6 | async-start | bytes 3145728 | tf_op jit(solution)/shard_map/all_to_all | solution.py:84
  394.1 45.9 %all-to-all-start.6 = ((bf16[64,2,48,1,128]{4,2,1,3,0:T(8,128)(2,1)}), bf16[64,2,48,1,128]{4,2,1,3,0:T(8,128)(2,1)}, u32[]{:S(2)}, u32[]{:S(2)}) async-start(bf16[64,2,48,1,128]{4,2,1,3,0:T(8,128)(2,1)} %fusion.13), calls=%async_computation.7 | async-start | bytes 3145728 | tf_op jit(solution)/shard_map/all_to_all | solution.py:110
  400.8 139.1 %reduce-scatter.5.cloned.1.call-start = ((), (), s32[]{:S(2)}) async-start(), calls=%async_computation.10 | async-start | bytes 1769472 | tf_op jit(solution)/shard_map/reduce_scatter | solution.py:133
  445.0 1.7 copy-start.3
Sparse Core Ops, SparseCore 0:
  196.1 90.8 reduce-scatter.2
  449.6 90.2 reduce-scatter.4
